TPU v7x, 32 devices: a whole 2x2x4 slice. The times are simulated.
32 devices in a mesh: ctx: 16 (over z, y, core), fsdp: 2 (over x).
Axes of the slice: x: 2, y: 2, z: 4, core: 2. Of those that a mesh axis runs over, the one named last changes fastest.
Arguments:
- tokens: bfloat16 [2, 4096, 768], P('fsdp', 'ctx'), may hold values from -6 to 6
- lengths: int32 [2], P('fsdp'), may hold values from 1024 to 4096, as said below
- cotangent: bfloat16 [2, 4096, 768], P('fsdp', 'ctx'), may hold values from -6 to 6
- query_weight: bfloat16 [768, 768], P('ctx', 'fsdp'), may hold values from -0.21875 to 0.21875
- key_weight: bfloat16 [768, 768], P('ctx', 'fsdp'), may hold values from -0.21875 to 0.21875
- value_weight: bfloat16 [768, 768], P('ctx', 'fsdp'), may hold values from -0.21875 to 0.21875
- out_weight: bfloat16 [768, 768], P('ctx', 'fsdp'), may hold values from -6 to 6
- in_weight: bfloat16 [768, 3072], P('ctx', 'fsdp'), may hold values from -0.21875 to 0.21875
- down_weight: bfloat16 [3072, 768], P('ctx', 'fsdp'), may hold values from -0.109375 to 0.109375
- query_bias: bfloat16 [768], P('ctx'), may hold values from -3 to 3
- value_bias: bfloat16 [768], P('ctx'), may hold values from -0.119628906 to 0.119628906
- out_bias: bfloat16 [768], P('ctx'), may hold values from -3 to 3
- attn_norm_gain: bfloat16 [768], P('ctx'), may hold values from 0.5 to 1.5
- attn_norm_bias: bfloat16 [768], P('ctx'), may hold values from -2 to 2
- in_bias: bfloat16 [3072], P('ctx'), may hold values from -3 to 3
- down_bias: bfloat16 [768], P('ctx'), may hold values from -3 to 3
- ffn_norm_gain: bfloat16 [768], P('ctx'), may hold values from 0.5 to 1.5
- ffn_norm_bias: bfloat16 [768], P('ctx'), may hold values from -2 to 2
Outputs:
- layer_out: bfloat16 [2, 4096, 768], P('fsdp', 'ctx')
- tokens_grad: bfloat16 [2, 4096, 768], P('fsdp', 'ctx')
- grad_query_weight: float32 [768, 768], P('ctx', 'fsdp')
- grad_key_weight: float32 [768, 768], P('ctx', 'fsdp')
- grad_value_weight: float32 [768, 768], P('ctx', 'fsdp')
- grad_out_weight: float32 [768, 768], P('ctx', 'fsdp')
- grad_in_weight: float32 [768, 3072], P('ctx', 'fsdp')
- grad_down_weight: float32 [3072, 768], P('ctx', 'fsdp')
- grad_query_bias: float32 [768], P('ctx')
- grad_value_bias: float32 [768], P('ctx')
- grad_out_bias: float32 [768], P('ctx')
- grad_attn_norm_gain: float32 [768], P('ctx')
- grad_attn_norm_bias: float32 [768], P('ctx')
- grad_in_bias: float32 [3072], P('ctx')
- grad_down_bias: float32 [768], P('ctx')
- grad_ffn_norm_gain: float32 [768], P('ctx')
- grad_ffn_norm_bias: float32 [768], P('ctx')
- rms_values: float32 [3], replicated
Inputs may be any that keep to these rules, and one draw needn't show every extreme that they name: `lengths`: each sequence has between 1024 and 4096 valid slots; some sequence has exactly 4096, another exactly 1024.
All inputs are finite; a program needn't handle non-finite values.
Results may differ from a plain program's by a relative error of at most 0.022.
Values may be sent and summed in bfloat16 or wider, within the bound.
No kernel may reach another device: no remote copies, remote signals or barrier semaphores. Data moves between devices by JAX's collectives and lax.ppermute only.
A program may use at most 192 MiB of HBM per device.

v0:
```python
import jax
import jax.numpy as jnp
from jax import lax
from jax.sharding import PartitionSpec as P

HEAD_DIM = 64
norm_eps = 1e-12
score_scale = 0.125
masked_score = -1000000000.0
rows_contract = (((0,), (0,)), ((), ()))
columns_contract = (((1,), (1,)), ((), ()))


def layer_norm(stream, gain_vec, shift_vec):
    center = jnp.mean(stream, axis=-1, keepdims=True)
    offset = stream - center
    spread = jnp.mean(offset * offset, axis=-1, keepdims=True)
    return offset * lax.rsqrt(spread + norm_eps) * gain_vec + shift_vec


def gelu_exact(inner_pre):
    return jax.nn.gelu(inner_pre, approximate=False)


def plain_product(left_side, right_side):
    return jnp.dot(left_side, right_side, preferred_element_type=jnp.float32)


def row_product(left_side, right_side):
    return lax.dot_general(left_side, right_side, rows_contract, preferred_element_type=jnp.float32)


def column_product(left_side, right_side):
    return lax.dot_general(
        left_side, right_side, columns_contract, preferred_element_type=jnp.float32
    )


def head_scores(query_head, key_head, key_ok):
    scores = (
        jnp.einsum("sqd,skd->sqk", query_head, key_head, preferred_element_type=jnp.float32)
        * score_scale
    )
    return jnp.where(key_ok[:, None, :], scores, masked_score)


def attend(query_seq, pair_all, key_ok):
    seq_count, slot_count, model_width = query_seq.shape
    heads_count = model_width // HEAD_DIM

    def one_head(head_index, loop_state):
        mixed_out, log_totals = loop_state
        head_start = head_index * HEAD_DIM
        query_head = lax.dynamic_slice_in_dim(query_seq, head_start, HEAD_DIM, 2)
        key_head = lax.dynamic_slice_in_dim(pair_all, head_start, HEAD_DIM, 2)
        value_head = lax.dynamic_slice_in_dim(pair_all, model_width + head_start, HEAD_DIM, 2)
        scores = head_scores(query_head, key_head, key_ok)
        row_peak = jnp.max(scores, axis=-1, keepdims=True)
        row_expo = jnp.exp(scores - row_peak)
        row_total = jnp.sum(row_expo, axis=-1, keepdims=True)
        attn_probs = (row_expo / row_total).astype(jnp.bfloat16)
        head_out = jnp.einsum(
            "sqk,skd->sqd", attn_probs, value_head, preferred_element_type=jnp.float32
        )
        mixed_out = lax.dynamic_update_slice_in_dim(mixed_out, head_out, head_start, 2)
        log_row = row_peak[..., 0] + jnp.log(row_total[..., 0])
        log_totals = lax.dynamic_update_index_in_dim(log_totals, log_row, head_index, 0)
        return (mixed_out, log_totals)

    start_state = (
        jnp.zeros((seq_count, slot_count, model_width), jnp.float32),
        jnp.zeros((heads_count, seq_count, slot_count), jnp.float32),
    )
    return lax.fori_loop(0, heads_count, one_head, start_state)


def attend_back(query_seq, pair_all, key_ok, log_totals, grad_mixed):
    seq_count, slot_count, model_width = query_seq.shape
    heads_count = model_width // HEAD_DIM

    def one_head(head_index, loop_state):
        grad_query, grad_pair = loop_state
        head_start = head_index * HEAD_DIM
        query_head = lax.dynamic_slice_in_dim(query_seq, head_start, HEAD_DIM, 2)
        key_head = lax.dynamic_slice_in_dim(pair_all, head_start, HEAD_DIM, 2)
        value_head = lax.dynamic_slice_in_dim(pair_all, model_width + head_start, HEAD_DIM, 2)
        grad_head = lax.dynamic_slice_in_dim(grad_mixed, head_start, HEAD_DIM, 2)
        scores = head_scores(query_head, key_head, key_ok)
        log_row = lax.dynamic_index_in_dim(log_totals, head_index, 0, keepdims=False)
        attn_probs = jnp.exp(scores - log_row[..., None])
        probs_b = attn_probs.astype(jnp.bfloat16)
        grad_probs = jnp.einsum(
            "sqd,skd->sqk", grad_head, value_head, preferred_element_type=jnp.float32
        )
        row_inner = jnp.sum(attn_probs * grad_probs, axis=-1, keepdims=True)
        grad_scores = (attn_probs * (grad_probs - row_inner)).astype(jnp.bfloat16)
        grad_query_head = (
            jnp.einsum("sqk,skd->sqd", grad_scores, key_head, preferred_element_type=jnp.float32)
            * score_scale
        )
        grad_key_head = (
            jnp.einsum("sqk,sqd->skd", grad_scores, query_head, preferred_element_type=jnp.float32)
            * score_scale
        )
        grad_value_head = jnp.einsum(
            "sqk,sqd->skd", probs_b, grad_head, preferred_element_type=jnp.float32
        )
        grad_query = lax.dynamic_update_slice_in_dim(grad_query, grad_query_head, head_start, 2)
        grad_pair = lax.dynamic_update_slice_in_dim(grad_pair, grad_key_head, head_start, 2)
        grad_pair = lax.dynamic_update_slice_in_dim(
            grad_pair, grad_value_head, model_width + head_start, 2
        )
        return (grad_query, grad_pair)

    start_state = (jnp.zeros(query_seq.shape, jnp.float32), jnp.zeros(pair_all.shape, jnp.float32))
    return lax.fori_loop(0, heads_count, one_head, start_state)


def column_sums(matrix_b):
    return jnp.sum(matrix_b.astype(jnp.float32), axis=0)


def body(
    tokens,
    lengths,
    cotangent,
    query_weight,
    key_weight,
    value_weight,
    out_weight,
    in_weight,
    down_weight,
    query_bias,
    value_bias,
    out_bias,
    attn_norm_gain,
    attn_norm_bias,
    in_bias,
    down_bias,
    ffn_norm_gain,
    ffn_norm_bias,
):
    seq_count, slot_count, model_width = tokens.shape
    row_count = seq_count * slot_count
    ctx_size = lax.axis_size("ctx")
    ctx_index = lax.axis_index("ctx")
    row_parts = (
        lax.all_gather(query_weight, "ctx", axis=0, tiled=True),
        lax.all_gather(key_weight, "ctx", axis=0, tiled=True),
        lax.all_gather(value_weight, "ctx", axis=0, tiled=True),
        lax.all_gather(out_weight, "ctx", axis=0, tiled=True),
        lax.all_gather(in_weight, "ctx", axis=0, tiled=True),
        lax.all_gather(down_weight, "ctx", axis=0, tiled=True),
        lax.all_gather(query_bias, "ctx", axis=0, tiled=True),
        lax.all_gather(value_bias, "ctx", axis=0, tiled=True),
        lax.all_gather(out_bias, "ctx", axis=0, tiled=True),
        lax.all_gather(attn_norm_gain, "ctx", axis=0, tiled=True),
        lax.all_gather(attn_norm_bias, "ctx", axis=0, tiled=True),
        lax.all_gather(in_bias, "ctx", axis=0, tiled=True),
        lax.all_gather(down_bias, "ctx", axis=0, tiled=True),
        lax.all_gather(ffn_norm_gain, "ctx", axis=0, tiled=True),
        lax.all_gather(ffn_norm_bias, "ctx", axis=0, tiled=True),
    )
    full_mats = (
        lax.all_gather(row_parts[0], "fsdp", axis=1, tiled=True),
        lax.all_gather(row_parts[1], "fsdp", axis=1, tiled=True),
        lax.all_gather(row_parts[2], "fsdp", axis=1, tiled=True),
        lax.all_gather(row_parts[3], "fsdp", axis=1, tiled=True),
        lax.all_gather(row_parts[4], "fsdp", axis=1, tiled=True),
        lax.all_gather(row_parts[5], "fsdp", axis=1, tiled=True),
    )
    query_full, key_full, value_full, out_full, in_full, down_full = full_mats
    query_vec = row_parts[6].astype(jnp.float32)
    value_vec = row_parts[7].astype(jnp.float32)
    out_vec = row_parts[8].astype(jnp.float32)
    gain_one = row_parts[9].astype(jnp.float32)
    bias_one = row_parts[10].astype(jnp.float32)
    in_vec = row_parts[11].astype(jnp.float32)
    down_vec = row_parts[12].astype(jnp.float32)
    gain_two = row_parts[13].astype(jnp.float32)
    bias_two = row_parts[14].astype(jnp.float32)
    local_slots = ctx_index * slot_count + jnp.arange(slot_count)
    local_ok = local_slots[None, :] < lengths[:, None]
    valid_mask = local_ok.astype(jnp.float32)
    valid_col = valid_mask.reshape(row_count, 1)
    key_ok = jnp.arange(slot_count * ctx_size)[None, :] < lengths[:, None]
    token_rows = tokens.reshape(row_count, model_width)
    queries_b = (plain_product(token_rows, query_full) + query_vec).astype(jnp.bfloat16)
    keys_b = plain_product(token_rows, key_full).astype(jnp.bfloat16)
    values_b = (plain_product(token_rows, value_full) + value_vec).astype(jnp.bfloat16)
    pair_local = jnp.concatenate([keys_b, values_b], axis=1).reshape(
        seq_count, slot_count, 2 * model_width
    )
    pair_all = lax.all_gather(pair_local, "ctx", axis=1, tiled=True)
    query_seq = queries_b.reshape(seq_count, slot_count, model_width)
    mixed_out, log_totals = attend(query_seq, pair_all, key_ok)
    mixed_b = mixed_out.reshape(row_count, model_width).astype(jnp.bfloat16)
    attn_branch = plain_product(mixed_b, out_full) + out_vec
    stream = token_rows.astype(jnp.float32) + attn_branch
    norm_one, norm_one_back = jax.vjp(layer_norm, stream, gain_one, bias_one)
    norm_one_b = norm_one.astype(jnp.bfloat16)
    inner_pre = plain_product(norm_one_b, in_full) + in_vec
    act_out, gelu_back = jax.vjp(gelu_exact, inner_pre)
    act_b = act_out.astype(jnp.bfloat16)
    ffn_branch = plain_product(act_b, down_full) + down_vec
    stream_two = norm_one + ffn_branch
    final_out, norm_two_back = jax.vjp(layer_norm, stream_two, gain_two, bias_two)
    layer_out = (
        (valid_col * final_out).astype(jnp.bfloat16).reshape(seq_count, slot_count, model_width)
    )
    grad_final = valid_col * cotangent.reshape(row_count, model_width).astype(jnp.float32)
    grad_stream_two, grad_gain_two, grad_bias_two = norm_two_back(grad_final)
    grad_ffn_b = grad_stream_two.astype(jnp.bfloat16)
    grad_down_vec = column_sums(grad_ffn_b)
    grad_down_full = row_product(act_b, grad_ffn_b)
    grad_inner_b = gelu_back(column_product(grad_ffn_b, down_full))[0].astype(jnp.bfloat16)
    grad_in_vec = column_sums(grad_inner_b)
    grad_in_full = row_product(norm_one_b, grad_inner_b)
    grad_norm_one = grad_stream_two + column_product(grad_inner_b, in_full)
    grad_stream, grad_gain_one, grad_bias_one = norm_one_back(grad_norm_one)
    grad_attn_b = grad_stream.astype(jnp.bfloat16)
    grad_out_vec = column_sums(grad_attn_b)
    grad_out_full = row_product(mixed_b, grad_attn_b)
    grad_mixed = (
        column_product(grad_attn_b, out_full)
        .astype(jnp.bfloat16)
        .reshape(seq_count, slot_count, model_width)
    )
    grad_query_seq, grad_pair = attend_back(query_seq, pair_all, key_ok, log_totals, grad_mixed)
    grad_pair_local = lax.psum_scatter(
        grad_pair.astype(jnp.bfloat16), "ctx", scatter_dimension=1, tiled=True
    ).astype(jnp.float32)
    grad_keys_b = (
        grad_pair_local[:, :, :model_width].reshape(row_count, model_width).astype(jnp.bfloat16)
    )
    grad_values_b = (
        grad_pair_local[:, :, model_width:].reshape(row_count, model_width).astype(jnp.bfloat16)
    )
    grad_queries_b = grad_query_seq.reshape(row_count, model_width).astype(jnp.bfloat16)
    grad_query_full = row_product(token_rows, grad_queries_b)
    grad_query_vec = column_sums(grad_queries_b)
    grad_key_full = row_product(token_rows, grad_keys_b)
    grad_value_full = row_product(token_rows, grad_values_b)
    grad_value_vec = column_sums(grad_values_b)
    tokens_grad = (
        (
            grad_stream
            + column_product(grad_queries_b, query_full)
            + column_product(grad_keys_b, key_full)
            + column_product(grad_values_b, value_full)
        )
        .astype(jnp.bfloat16)
        .reshape(seq_count, slot_count, model_width)
    )
    narrow = (
        lax.psum_scatter(
            grad_query_full.astype(jnp.bfloat16), "fsdp", scatter_dimension=1, tiled=True
        ).astype(jnp.float32),
        lax.psum_scatter(
            grad_key_full.astype(jnp.bfloat16), "fsdp", scatter_dimension=1, tiled=True
        ).astype(jnp.float32),
        lax.psum_scatter(
            grad_value_full.astype(jnp.bfloat16), "fsdp", scatter_dimension=1, tiled=True
        ).astype(jnp.float32),
        lax.psum_scatter(
            grad_out_full.astype(jnp.bfloat16), "fsdp", scatter_dimension=1, tiled=True
        ).astype(jnp.float32),
        lax.psum_scatter(
            grad_in_full.astype(jnp.bfloat16), "fsdp", scatter_dimension=1, tiled=True
        ).astype(jnp.float32),
        lax.psum_scatter(
            grad_down_full.astype(jnp.bfloat16), "fsdp", scatter_dimension=1, tiled=True
        ).astype(jnp.float32),
    )
    owned_grads = (
        lax.psum_scatter(
            narrow[0].astype(jnp.bfloat16), "ctx", scatter_dimension=0, tiled=True
        ).astype(jnp.float32),
        lax.psum_scatter(
            narrow[1].astype(jnp.bfloat16), "ctx", scatter_dimension=0, tiled=True
        ).astype(jnp.float32),
        lax.psum_scatter(
            narrow[2].astype(jnp.bfloat16), "ctx", scatter_dimension=0, tiled=True
        ).astype(jnp.float32),
        lax.psum_scatter(
            narrow[3].astype(jnp.bfloat16), "ctx", scatter_dimension=0, tiled=True
        ).astype(jnp.float32),
        lax.psum_scatter(
            narrow[4].astype(jnp.bfloat16), "ctx", scatter_dimension=0, tiled=True
        ).astype(jnp.float32),
        lax.psum_scatter(
            narrow[5].astype(jnp.bfloat16), "ctx", scatter_dimension=0, tiled=True
        ).astype(jnp.float32),
    )
    moments = jnp.stack(
        [
            jnp.sum(valid_col * stream * stream),
            jnp.sum(valid_col * attn_branch * attn_branch),
            jnp.sum(valid_col * ffn_branch * ffn_branch),
            jnp.sum(valid_col),
        ]
    )
    summed = lax.psum(
        (
            moments,
            grad_query_vec,
            grad_value_vec,
            grad_out_vec,
            grad_gain_one,
            grad_bias_one,
            grad_in_vec,
            grad_down_vec,
            grad_gain_two,
            grad_bias_two,
        ),
        ("ctx", "fsdp"),
    )
    width_shard = query_bias.shape[0]
    hidden_shard = in_bias.shape[0]

    def own_piece(vector_full, shard_len):
        return lax.dynamic_slice_in_dim(vector_full, ctx_index * shard_len, shard_len, 0)

    rms_values = jnp.sqrt(summed[0][:3] / (summed[0][3] * model_width))
    return (
        layer_out,
        tokens_grad,
        owned_grads[0],
        owned_grads[1],
        owned_grads[2],
        owned_grads[3],
        owned_grads[4],
        owned_grads[5],
        own_piece(summed[1], width_shard),
        own_piece(summed[2], width_shard),
        own_piece(summed[3], width_shard),
        own_piece(summed[4], width_shard),
        own_piece(summed[5], width_shard),
        own_piece(summed[6], hidden_shard),
        own_piece(summed[7], width_shard),
        own_piece(summed[8], width_shard),
        own_piece(summed[9], width_shard),
        rms_values,
    )


def solution(mesh):
    in_specs = (
        P("fsdp", "ctx", None),
        P("fsdp"),
        P("fsdp", "ctx", None),
        P("ctx", "fsdp"),
        P("ctx", "fsdp"),
        P("ctx", "fsdp"),
        P("ctx", "fsdp"),
        P("ctx", "fsdp"),
        P("ctx", "fsdp"),
        P("ctx"),
        P("ctx"),
        P("ctx"),
        P("ctx"),
        P("ctx"),
        P("ctx"),
        P("ctx"),
        P("ctx"),
        P("ctx"),
    )
    out_specs = (
        P("fsdp", "ctx", None),
        P("fsdp", "ctx", None),
        P("ctx", "fsdp"),
        P("ctx", "fsdp"),
        P("ctx", "fsdp"),
        P("ctx", "fsdp"),
        P("ctx", "fsdp"),
        P("ctx", "fsdp"),
        P("ctx"),
        P("ctx"),
        P("ctx"),
        P("ctx"),
        P("ctx"),
        P("ctx"),
        P("ctx"),
        P("ctx"),
        P("ctx"),
        P(),
    )
    return jax.shard_map(body, mesh=mesh, in_specs=in_specs, out_specs=out_specs, check_vma=False)
```

profile of v0, /device:TPU:0, one launch (start us, length us, event | category | flops | bytes accessed | tf_op | source)
XLA Modules:
  0.0 1333.6 jit_solution(6212013291559108767)
XLA Ops:
  7.4 26.6 %all_gather.69 = bf16[768,384]{1,0:T(8,128)(2,1)} all-gather(bf16[48,384]{1,0:T(8,128)(2,1)} %param.26), channel_id=1, replica_groups=mesh['ctx'=16,'fsdp'=2] {'ctx'}, dimensions={0}, use_global_device_ids=true | all-gather | bytes 626688 | tf_op jit(solution)/shard_map/all_gather | solution.py:149
  34.1 20.7 %all_gather.71 = bf16[768,384]{1,0:T(8,128)(2,1)} all-gather(bf16[48,384]{1,0:T(8,128)(2,1)} %param.27), channel_id=1, replica_groups=mesh['ctx'=16,'fsdp'=2] {'ctx'}, dimensions={0}, use_global_device_ids=true | all-gather | bytes 626688 | tf_op jit(solution)/shard_map/all_gather | solution.py:150
  55.6 22.2 %all_gather.66 = bf16[768,384]{1,0:T(8,128)(2,1)} all-gather(bf16[48,384]{1,0:T(8,128)(2,1)} %param.25), channel_id=1, replica_groups=mesh['ctx'=16,'fsdp'=2] {'ctx'}, dimensions={0}, use_global_device_ids=true | all-gather | bytes 626688 | tf_op jit(solution)/shard_map/all_gather | solution.py:148
  82.5 58.1 %all-reduce.10 = (bf16[768]{0:T(1024)(128)(2,1)S(1)}, bf16[768]{0:T(1024)(128)(2,1)S(1)}, bf16[3072]{0:T(1024)(128)(2,1)S(1)}, bf16[768]{0:T(1024)(128)(2,1)S(1)...) all-reduce(bf16[768]{0:T(1024)(128)(2,1)S(1)} %dynamic-update-slice, ...), channel_id=1, replica_groups=mesh['ctx'=16,'fsdp'=2] {'ctx'}, use_global_device_ids=true, to_apply=%add | all-reduce | flops 9216 | bytes 36864
  145.2 20.6 %all_gather.75 = bf16[768,384]{1,0:T(8,128)(2,1)} all-gather(bf16[48,384]{1,0:T(8,128)(2,1)S(1)} %copy-done.13), channel_id=1, replica_groups=mesh['ctx'=16,'fsdp'=2] {'ctx'}, dimensions={0}, use_global_device_ids=true | all-gather | bytes 626688 | tf_op jit(solution)/shard_map/all_gather | solution.py:151
  169.1 21.9 %all-gather.23.cloned.1.call-done = bf16[3072,384]{1,0:T(8,128)(2,1)} async-done(((bf16[192,384]{1,0:T(8,128)(2,1)}), bf16[3072,384]{1,0:T(8,128)(2,1)}) %all-gather.23.cloned.1.call-update) | async-done | bytes 2359312 | tf_op jit(solution)/shard_map/all_gather | solution.py:153
  191.4 101.4 %all-gather.27.cloned.1.call-done = bf16[4096,1536]{1,0:T(8,128)(2,1)} async-done(((bf16[256,1536]{1,0:T(8,128)(2,1)}), bf16[4096,1536]{1,0:T(8,128)(2,1)}) %all-gather.27.cloned.1.call-update) | async-done | bytes 12582928 | tf_op jit(solution)/shard_map/all_gather | solution.py:194
  292.8 77.5 %while.36 = (s32[]{:T(128)}, bf16[1,256,768]{1,2,0:T(8,128)(2,1)S(1)}, f32[12,1,256]{2,1,0:T(1,128)S(1)}, bf16[1,256,768]{2,1,0:T(8,128)(2,1)S(1)}, bf16[1,4096,...) while((s32[]{:T(128)}, ...), condition=%wide.region_3.4_spmd.clone, body=%wide.region_0.3_spmd.clone.sunk | while | flops 276827904 | bytes 14829822 | solution.py:74
  322.3 2.9 fusion.147
  328.9 2.8 fusion.147
  372.6 6.9 all-gather.21.cloned.1.call-done
  379.5 12.1 multiply_convert_fusion.1
  391.6 52.1 %all-gather.25.cloned.1.call-done = bf16[3072,768]{1,0:T(8,128)(2,1)} async-done(((bf16[3072,384]{1,0:T(8,128)(2,1)}), bf16[3072,768]{1,0:T(8,128)(2,1)}) %all-gather.25.cloned.1.call-update) | async-done | bytes 4718608 | tf_op jit(solution)/shard_map/all_gather | solution.py:170
  443.8 4.4 fusion.101
  451.8 2.7 convert_reduce_fusion
  458.8 6.1 broadcast_in_dim.102
  464.8 142.2 %while.37 = (s32[]{:T(128)}, bf16[1,256,768]{1,2,0:T(8,128)(2,1)S(1)}, bf16[1,4096,1536]{1,2,0:T(8,128)(2,1)}, bf16[1,256,768]{2,1,0:T(8,128)(2,1)S(1)}, bf16[1,...) while((s32[]{:T(128)}, ...), condition=%wide.region_14.15_spmd.clone, body=%wide.region_12.14_spmd.clone.sunk | while | flops 680808192 | bytes 37041444 | solution.py:116
  467.8 2.8 multiply_reduce_fusion.6
  479.6 2.7 multiply_reduce_fusion.6
  491.5 2.8 multiply_reduce_fusion.6
  503.3 2.8 multiply_reduce_fusion.6
  515.1 2.7 multiply_reduce_fusion.6
  526.9 2.7 multiply_reduce_fusion.6
  538.8 2.7 multiply_reduce_fusion.6
  550.6 2.7 multiply_reduce_fusion.6
  562.5 2.8 multiply_reduce_fusion.6
  574.3 2.8 multiply_reduce_fusion.6
  586.1 2.8 multiply_reduce_fusion.6
  598.0 2.8 multiply_reduce_fusion.6
  611.9 5.7 convolution_convert_fusion.1
  619.4 3.7 convolution_convert_fusion
  623.1 7.1 copy.50
  630.3 111.7 %reduce-scatter.24.cloned.1.call-done = bf16[1,256,1536]{1,2,0:T(8,128)(2,1)} async-done(((bf16[1,4096,1536]{1,2,0:T(8,128)(2,1)}), bf16[1,256,1536]{1,2,0:T(8,128)(2,1)}) %reduce-scatter.24.cloned.1.call-update) | async-done | bytes 786448 | tf_op jit(solution)/shard_map/reduce_scatter | solution.py:230
  744.6 20.6 %reduce-scatter.26.cloned.1.call-done = bf16[768,384]{0,1:T(8,128)(2,1)} async-done(((bf16[768,768]{0,1:T(8,128)(2,1)}), bf16[768,384]{0,1:T(8,128)(2,1)}) %reduce-scatter.26.cloned.1.call-update) | async-done | bytes 589840 | tf_op jit(solution)/shard_map/reduce_scatter | solution.py:256
  767.4 21.8 %reduce-scatter.46.cloned.1.call-done = bf16[384,768]{1,0:T(8,128)(2,1)} async-done(((bf16[768,768]{1,0:T(8,128)(2,1)}), bf16[384,768]{1,0:T(8,128)(2,1)}) %reduce-scatter.46.cloned.1.call-update) | async-done | bytes 589840
  791.4 60.1 %reduce-scatter.34.cloned.1.call-done = bf16[768,1536]{1,0:T(8,128)(2,1)} async-done(((bf16[768,3072]{1,0:T(8,128)(2,1)}), bf16[768,1536]{1,0:T(8,128)(2,1)}) %reduce-scatter.34.cloned.1.call-update) | async-done | bytes 2359312 | tf_op jit(solution)/shard_map/reduce_scatter | solution.py:268
  851.5 62.2 %reduce-scatter.48.cloned.1.call-done = bf16[384,3072]{1,0:T(8,128)(2,1)} async-done(((bf16[768,3072]{1,0:T(8,128)(2,1)}), bf16[384,3072]{1,0:T(8,128)(2,1)}) %reduce-scatter.48.cloned.1.call-update) | async-done | bytes 2359312
  913.8 4.4 copy.51
  919.8 17.8 %reduce-scatter.28.cloned.1.call-done = bf16[768,384]{0,1:T(8,128)(2,1)} async-done(((bf16[768,768]{0,1:T(8,128)(2,1)}), bf16[768,384]{0,1:T(8,128)(2,1)}) %reduce-scatter.28.cloned.1.call-update) | async-done | bytes 589840 | tf_op jit(solution)/shard_map/reduce_scatter | solution.py:259
  943.6 2.8 convolution_add_fusion.3
  946.4 49.9 %reduce-scatter.40.cloned.1.call-done = bf16[48,384]{1,0:T(8,128)(2,1)} async-done(((bf16[768,384]{1,0:T(8,128)(2,1)}), bf16[48,384]{1,0:T(8,128)(2,1)}) %reduce-scatter.40.cloned.1.call-update) | async-done | bytes 36880
  998.0 55.7 %reduce-scatter.32.cloned.1.call-done = bf16[48,384]{1,0:T(8,128)(2,1)} async-done(((bf16[768,384]{1,0:T(8,128)(2,1)}), bf16[48,384]{1,0:T(8,128)(2,1)}) %reduce-scatter.32.cloned.1.call-update) | async-done | bytes 36880 | tf_op jit(solution)/shard_map/reduce_scatter | solution.py:285
  1055.0 64.8 %reduce-scatter.36.cloned.1.call-done = bf16[48,1536]{1,0:T(8,128)(2,1)} async-done(((bf16[768,1536]{1,0:T(8,128)(2,1)}), bf16[48,1536]{1,0:T(8,128)(2,1)}) %reduce-scatter.36.cloned.1.call-update) | async-done | bytes 147472 | tf_op jit(solution)/shard_map/reduce_scatter | solution.py:288
  1121.5 64.1 %reduce-scatter.38.cloned.1.call-done = bf16[192,384]{1,0:T(8,128)(2,1)} async-done(((bf16[3072,384]{1,0:T(8,128)(2,1)}), bf16[192,384]{1,0:T(8,128)(2,1)}) %reduce-scatter.38.cloned.1.call-update) | async-done | bytes 147472 | tf_op jit(solution)/shard_map/reduce_scatter | solution.py:291
  1187.2 21.3 %reduce-scatter.30.cloned.1.call-done = bf16[768,384]{0,1:T(8,128)(2,1)} async-done(((bf16[768,768]{0,1:T(8,128)(2,1)}), bf16[768,384]{0,1:T(8,128)(2,1)}) %reduce-scatter.30.cloned.1.call-update) | async-done | bytes 589840 | tf_op jit(solution)/shard_map/reduce_scatter | solution.py:262
  1210.9 40.5 %all-reduce.9 = (f32[768]{0:T(1024)S(1)}, f32[768]{0:T(1024)S(1)}, f32[768]{0:T(1024)S(1)}, f32[768]{0:T(1024)S(1)}, f32[768]{0:T(1024)S(1)}, /*index=5*/f32[307...) all-reduce(f32[768]{0:T(1024)S(1)} %convert_reduce_fusion.4, ...), channel_id=1, replica_groups=mesh['ctx'=16,'fsdp'=2] {'ctx','fsdp'}, use_global_device_ids=true, to_apply=%region_29.30 | all-reduce | flops 9220 | bytes 73760 | tf_op jit(solution)/shard_map/psum | solution.py:303
  1260.3 6.8 reduce-scatter.42.cloned.1.call-done
  1268.7 56.3 %reduce-scatter.44.cloned.1.call-done = bf16[48,384]{1,0:T(8,128)(2,1)} async-done(((bf16[768,384]{1,0:T(8,128)(2,1)}), bf16[48,384]{1,0:T(8,128)(2,1)}) %reduce-scatter.44.cloned.1.call-update) | async-done | bytes 36880
  (367 shorter events, 242.9 us)
Async XLA Ops:
  7.2 71.3 %copy-start.32 = (u32[32]{0:T(128)S(1)}, u32[32]{0:T(128)}, u32[]{:S(2)}) copy-start(u32[32]{0:T(128)} %constant.307) | copy-start | bytes 388
  7.2 73.1 %copy-start.23 = (bf16[48]{0:T(256)(128)(2,1)S(1)}, bf16[48]{0:T(256)(128)(2,1)}, u32[]{:S(2)}) copy-start(bf16[48]{0:T(256)(128)(2,1)} %param.38) | copy-start | bytes 292
  7.2 73.4 %copy-start.24 = (bf16[48]{0:T(256)(128)(2,1)S(1)}, bf16[48]{0:T(256)(128)(2,1)}, u32[]{:S(2)}) copy-start(bf16[48]{0:T(256)(128)(2,1)} %param.37) | copy-start | bytes 292
  7.2 73.6 %copy-start.25 = (bf16[48]{0:T(256)(128)(2,1)S(1)}, bf16[48]{0:T(256)(128)(2,1)}, u32[]{:S(2)}) copy-start(bf16[48]{0:T(256)(128)(2,1)} %param.34) | copy-start | bytes 292
  7.2 73.8 %copy-start.26 = (bf16[48]{0:T(256)(128)(2,1)S(1)}, bf16[48]{0:T(256)(128)(2,1)}, u32[]{:S(2)}) copy-start(bf16[48]{0:T(256)(128)(2,1)} %param.35) | copy-start | bytes 292
  7.2 74.1 %copy-start.27 = (bf16[48]{0:T(256)(128)(2,1)S(1)}, bf16[48]{0:T(256)(128)(2,1)}, u32[]{:S(2)}) copy-start(bf16[48]{0:T(256)(128)(2,1)} %param.33) | copy-start | bytes 292
  7.3 74.3 %copy-start.28 = (bf16[48]{0:T(256)(128)(2,1)S(1)}, bf16[48]{0:T(256)(128)(2,1)}, u32[]{:S(2)}) copy-start(bf16[48]{0:T(256)(128)(2,1)} %param.32) | copy-start | bytes 292
  7.3 74.5 %copy-start.29 = (bf16[48]{0:T(256)(128)(2,1)S(1)}, bf16[48]{0:T(256)(128)(2,1)}, u32[]{:S(2)}) copy-start(bf16[48]{0:T(256)(128)(2,1)} %param.31) | copy-start | bytes 292
  7.3 74.7 %copy-start.30 = (bf16[48]{0:T(256)(128)(2,1)S(1)}, bf16[48]{0:T(256)(128)(2,1)}, u32[]{:S(2)}) copy-start(bf16[48]{0:T(256)(128)(2,1)} %param.39) | copy-start | bytes 292
  7.3 75.0 %copy-start.31 = (bf16[192]{0:T(256)(128)(2,1)S(1)}, bf16[192]{0:T(256)(128)(2,1)}, u32[]{:S(2)}) copy-start(bf16[192]{0:T(256)(128)(2,1)} %param.36) | copy-start | bytes 1156
  7.3 133.3 %copy-start = (bf16[1,256,768]{2,1,0:T(8,128)(2,1)S(1)}, bf16[1,256,768]{2,1,0:T(8,128)(2,1)}, u32[]{:S(2)}) copy-start(bf16[1,256,768]{2,1,0:T(8,128)(2,1)} %param.22) | copy-start | bytes 1179652
  7.3 133.3 %all-gather.13.cloned.1.call-start = ((), (), s32[]{:S(2)}) async-start(), calls=%async_computation.14 | async-start | bytes 1769472 | tf_op jit(solution)/shard_map/all_gather | solution.py:166
  34.0 108.4 %all-gather.15.cloned.1.call-start = ((), (), s32[]{:S(2)}) async-start(), calls=%async_computation.15 | async-start | bytes 1769472 | tf_op jit(solution)/shard_map/all_gather | solution.py:167
  54.8 111.1 %all-gather.19.cloned.1.call-start = ((), (), s32[]{:S(2)}) async-start(), calls=%async_computation.17 | async-start | bytes 2506752 | tf_op jit(solution)/shard_map/all_gather | solution.py:152
  55.5 111.9 %all-gather.11.cloned.1.call-start = ((), (), s32[]{:S(2)}) async-start(), calls=%async_computation.13 | async-start | bytes 1769472 | tf_op jit(solution)/shard_map/all_gather | solution.py:165
  77.8 113.3 %all-gather.23.cloned.1.call-start = ((), (), s32[]{:S(2)}) async-start(), calls=%async_computation.19 | async-start | bytes 2506752 | tf_op jit(solution)/shard_map/all_gather | solution.py:153
  78.4 214.4 %all-gather.27.cloned.1.call-start = ((), (), s32[]{:S(2)}) async-start(), calls=%async_computation.29 | async-start | bytes 13369344 | tf_op jit(solution)/shard_map/all_gather | solution.py:194
  140.6 4.6 copy-start.13
  145.1 225.2 %all-gather.17.cloned.1.call-start = ((), (), s32[]{:S(2)}) async-start(), calls=%async_computation.16 | async-start | bytes 1769472 | tf_op jit(solution)/shard_map/all_gather | solution.py:168
  165.8 213.7 %all-gather.21.cloned.1.call-start = ((), (), s32[]{:S(2)}) async-start(), calls=%async_computation.18 | async-start | bytes 7077888 | tf_op jit(solution)/shard_map/all_gather | solution.py:169
  166.5 277.2 %all-gather.25.cloned.1.call-start = ((), (), s32[]{:S(2)}) async-start(), calls=%async_computation.20 | async-start | bytes 7077888 | tf_op jit(solution)/shard_map/all_gather | solution.py:170
  191.1 550.9 %reduce-scatter.24.cloned.1.call-start = ((), (), s32[]{:S(2)}) async-start(), calls=%async_computation.21 | async-start | bytes 13369344 | tf_op jit(solution)/shard_map/reduce_scatter | solution.py:230
  370.3 21.3 %copy-start.4 = (bf16[1,256,768]{1,2,0:T(8,128)(2,1)}, bf16[1,256,768]{1,2,0:T(8,128)(2,1)S(1)}, u32[]{:S(2)}) copy-start(bf16[1,256,768]{1,2,0:T(8,128)(2,1)S(1)} %get-tuple-element.372) | copy-start | bytes 1179652
  372.6 84.3 %copy-start.17 = (f32[256]{0:T(256)}, f32[256]{0:T(256)S(1)}, u32[]{:S(2)}) copy-start(f32[256]{0:T(256)S(1)} %fusion.90) | copy-start | bytes 3076
  443.8 4.7 copy-start.10
  443.8 8.0 copy-start.33
  443.8 8.0 copy-start.34
  607.1 158.1 %reduce-scatter.26.cloned.1.call-start = ((), (), s32[]{:S(2)}) async-start(), calls=%async_computation.22 | async-start | bytes 1769472 | tf_op jit(solution)/shard_map/reduce_scatter | solution.py:256
  608.7 180.4 %reduce-scatter.46.cloned.1.call-start = ((), (), s32[]{:S(2)}) async-start(), calls=%async_computation.33 | async-start | bytes 1769472
  611.8 239.6 %reduce-scatter.34.cloned.1.call-start = ((), (), s32[]{:S(2)}) async-start(), calls=%async_computation.26 | async-start | bytes 7077888 | tf_op jit(solution)/shard_map/reduce_scatter | solution.py:268
  617.6 296.1 %reduce-scatter.48.cloned.1.call-start = ((), (), s32[]{:S(2)}) async-start(), calls=%async_computation.34 | async-start | bytes 7077888
  630.3 307.4 %reduce-scatter.28.cloned.1.call-start = ((), (), s32[]{:S(2)}) async-start(), calls=%async_computation.23 | async-start | bytes 1769472 | tf_op jit(solution)/shard_map/reduce_scatter | solution.py:259
  744.5 251.9 %reduce-scatter.40.cloned.1.call-start = ((), (), s32[]{:S(2)}) async-start(), calls=%async_computation.30 | async-start | bytes 626688
  767.3 286.3 %reduce-scatter.32.cloned.1.call-start = ((), (), s32[]{:S(2)}) async-start(), calls=%async_computation.25 | async-start | bytes 626688 | tf_op jit(solution)/shard_map/reduce_scatter | solution.py:285
  791.3 328.5 %reduce-scatter.36.cloned.1.call-start = ((), (), s32[]{:S(2)}) async-start(), calls=%async_computation.27 | async-start | bytes 2506752 | tf_op jit(solution)/shard_map/reduce_scatter | solution.py:288
  851.5 334.1 %reduce-scatter.38.cloned.1.call-start = ((), (), s32[]{:S(2)}) async-start(), calls=%async_computation.28 | async-start | bytes 2506752 | tf_op jit(solution)/shard_map/reduce_scatter | solution.py:291
  918.1 290.4 %reduce-scatter.30.cloned.1.call-start = ((), (), s32[]{:S(2)}) async-start(), calls=%async_computation.24 | async-start | bytes 1769472 | tf_op jit(solution)/shard_map/reduce_scatter | solution.py:262
  919.8 347.3 %reduce-scatter.42.cloned.1.call-start = ((), (), s32[]{:S(2)}) async-start(), calls=%async_computation.31 | async-start | bytes 626688
  939.8 385.1 %reduce-scatter.44.cloned.1.call-start = ((), (), s32[]{:S(2)}) async-start(), calls=%async_computation.32 | async-start | bytes 626688
  943.5 267.3 %copy-start.14 = (f32[768]{0:T(1024)S(1)}, f32[768]{0:T(1024)}, u32[]{:S(2)}) copy-start(f32[768]{0:T(1024)} %get-tuple-element.457) | copy-start | bytes 9220
  943.5 267.3 %copy-start.15 = (f32[768]{0:T(1024)S(1)}, f32[768]{0:T(1024)}, u32[]{:S(2)}) copy-start(f32[768]{0:T(1024)} %get-tuple-element.505) | copy-start | bytes 9220
  943.5 267.3 %copy-start.16 = (f32[768]{0:T(1024)S(1)}, f32[768]{0:T(1024)}, u32[]{:S(2)}) copy-start(f32[768]{0:T(1024)} %get-tuple-element.509) | copy-start | bytes 9220
  943.6 267.3 %copy-start.18 = (f32[3072]{0:T(1024)S(1)}, f32[3072]{0:T(1024)}, u32[]{:S(2)}) copy-start(f32[3072]{0:T(1024)} %get-tuple-element.507) | copy-start | bytes 36868
  943.6 267.3 %copy-start.20 = (f32[768]{0:T(1024)S(1)}, f32[768]{0:T(1024)}, u32[]{:S(2)}) copy-start(f32[768]{0:T(1024)} %get-tuple-element.446) | copy-start | bytes 9220
  943.6 267.3 %copy-start.21 = (f32[768]{0:T(1024)S(1)}, f32[768]{0:T(1024)}, u32[]{:S(2)}) copy-start(f32[768]{0:T(1024)} %get-tuple-element.451) | copy-start | bytes 9220
  943.6 314.9 %copy-start.2 = (bf16[768,768]{1,0:T(8,128)(2,1)S(1)}, bf16[768,768]{1,0:T(8,128)(2,1)}, u32[]{:S(2)}) copy-start(bf16[768,768]{1,0:T(8,128)(2,1)} %all-gather.13.cloned.1.call-done) | copy-start | bytes 3538948
  946.4 312.0 %copy-start.7 = (f32[256,768]{1,0:T(8,128)S(1)}, f32[256,768]{1,0:T(8,128)}, u32[]{:S(2)}) copy-start(f32[256,768]{1,0:T(8,128)} %convolution_add_fusion.3) | copy-start | bytes 2359300
  1251.4 7.6 copy-start.12
  (11 other events, 25.3 us)
Sparse Core Ops, SparseCore 0:
  34.1 20.0 all-gather.12
  55.8 22.7 all-gather.14
  80.9 42.4 all-gather.18
  124.7 21.5 all-gather.10
  148.5 42.5 all-gather.22
  193.2 99.5 all-gather.26
  294.3 20.9 all-gather.16
  316.8 62.6 all-gather.20
  381.1 62.6 all-gather.24
  607.2 134.7 reduce-scatter.23
  744.2 20.8 reduce-scatter.25
  767.4 21.7 reduce-scatter.45
  791.4 59.9 reduce-scatter.33
  853.7 59.9 reduce-scatter.47
  915.9 21.7 reduce-scatter.27
  941.5 54.8 reduce-scatter.39
  999.8 53.8 reduce-scatter.31
  1057.7 62.0 reduce-scatter.35
  1123.6 61.9 reduce-scatter.37
  1187.7 20.7 reduce-scatter.29
  1212.1 54.9 reduce-scatter.41
  1271.0 53.8 reduce-scatter.43
where the time goes:
time: 1340 us; the launch traced here: 1330 us
  waiting for transfers between devices  798 us (60%)
  matrix products  232 us (17%)
  blocking collectives  189 us (14%)
  other arithmetic  51.6 us (4%)
  local copies, waits for them, and re-layouts  43.3 us (3%)
  between operations  17.8 us (1%)
    unnamed x27, waiting for transfers between devices  199 us
    reduce_scatter x1, waiting for transfers between devices, body(): lax.psum_scatter(grad_pair.astype(jnp.bfloat16), 'ctx', scatter_dimension...  112 us
    all_gather x1, waiting for transfers between devices, body(): pair_all = lax.all_gather(pair_local, 'ctx', axis=1, tiled=True)  101 us
    reduce_scatter x1, waiting for transfers between devices, body(): lax.psum_scatter(narrow[4].astype(jnp.bfloat16), 'ctx', scatter_dimension...  64.8 us
    reduce_scatter x1, waiting for transfers between devices, body(): lax.psum_scatter(narrow[5].astype(jnp.bfloat16), 'ctx', scatter_dimension...  64.1 us
    reduce_scatter x1, waiting for transfers between devices, body(): lax.psum_scatter(grad_in_full.astype(jnp.bfloat16), 'fsdp', scatter_dimen...  60.1 us
    dot_general x24, matrix products, head_scores(): jnp.einsum('sqd,skd->sqk', query_head, key_head, preferred_element_type=j...  59.8 us
    unnamed x1, blocking collectives  58.1 us
  transfers between devices with their start and end apart: 22, of which 17 were waited for; matrix products, arithmetic and copies ran while one was open for 12% of the time, Pallas kernels for 0%

commit v1 on v0

--- a/solution.py
+++ b/solution.py
@@ -161,13 +161,29 @@
         lax.all_gather(ffn_norm_gain, "ctx", axis=0, tiled=True),
         lax.all_gather(ffn_norm_bias, "ctx", axis=0, tiled=True),
     )
+
+    def report_domain_over_axis(obj, net_axis):
+        current_block, left_arr = (lax.axis_size(net_axis), lax.axis_index(net_axis))
+        far_arr, block_next = (obj, 1)
+        while block_next < current_block:
+            piece_next = lax.ppermute(
+                far_arr,
+                axis_name=net_axis,
+                perm=tuple(((dev_i, dev_i ^ block_next) for dev_i in range(current_block))),
+            )
+            z = jnp.concatenate([far_arr, piece_next], 1)
+            step_out = jnp.concatenate([piece_next, far_arr], 1)
+            far_arr = jnp.where(left_arr & block_next == 0, z, step_out)
+            block_next = 2 * block_next
+        return far_arr
+
     full_mats = (
         lax.all_gather(row_parts[0], "fsdp", axis=1, tiled=True),
         lax.all_gather(row_parts[1], "fsdp", axis=1, tiled=True),
         lax.all_gather(row_parts[2], "fsdp", axis=1, tiled=True),
         lax.all_gather(row_parts[3], "fsdp", axis=1, tiled=True),
         lax.all_gather(row_parts[4], "fsdp", axis=1, tiled=True),
-        lax.all_gather(row_parts[5], "fsdp", axis=1, tiled=True),
+        report_domain_over_axis(row_parts[5], "fsdp"),
     )
     query_full, key_full, value_full, out_full, in_full, down_full = full_mats
     query_vec = row_parts[6].astype(jnp.float32)

time: 1340 us -> 1290 us (0.963)
  waiting for transfers between devices: 798 us -> 744 us
    all_gather x1 -> x0, waiting for transfers between devices: 52.1 us -> none  [body(): lax.all_gather(row_parts[5], 'fsdp', axis=1, tiled=True)]
    all_gather x1, waiting for transfers between devices: 21.9 us -> 0.02 us  [body(): lax.all_gather(down_weight, 'ctx', axis=0, tiled=True)]
    all_gather x1, waiting for transfers between devices: 0.02 us -> 21.1 us  [body(): lax.all_gather(in_weight, 'ctx', axis=0, tiled=True)]
    unnamed x27 -> x26, waiting for transfers between devices: 199 us -> 199 us
    unnamed x106 -> x104, local copies, waits for them, and re-layouts: 31.1 us -> 30.8 us
  transfers between devices with their start and end apart: 22 -> 22, of which waited for: 17 -> 16; matrix products, arithmetic and copies ran while one was open for 12% -> 12% of each run, Pallas kernels for 0% -> 0%
where the time goes in v1:
time: 1290 us; the launch traced here: 1280 us
  waiting for transfers between devices  744 us (58%)
  matrix products  233 us (18%)
  blocking collectives  189 us (15%)
  other arithmetic  51.6 us (4%)
  local copies, waits for them, and re-layouts  43 us (3%)
  between operations  17.9 us (1%)
    unnamed x26, waiting for transfers between devices  199 us
    reduce_scatter x1, waiting for transfers between devices, body(): lax.psum_scatter(grad_pair.astype(jnp.bfloat16), 'ctx', scatter_dimension...  112 us
    all_gather x1, waiting for transfers between devices, body(): pair_all = lax.all_gather(pair_local, 'ctx', axis=1, tiled=True)  102 us
    reduce_scatter x1, waiting for transfers between devices, body(): lax.psum_scatter(narrow[4].astype(jnp.bfloat16), 'ctx', scatter_dimension...  64.7 us
    reduce_scatter x1, waiting for transfers between devices, body(): lax.psum_scatter(narrow[5].astype(jnp.bfloat16), 'ctx', scatter_dimension...  64 us
    reduce_scatter x1, waiting for transfers between devices, body(): lax.psum_scatter(grad_in_full.astype(jnp.bfloat16), 'fsdp', scatter_dimen...  60 us
    dot_general x24, matrix products, head_scores(): jnp.einsum('sqd,skd->sqk', query_head, key_head, preferred_element_type=j...  59.8 us
    unnamed x1, blocking collectives  58 us
  transfers between devices with their start and end apart: 22, of which 16 were waited for; matrix products, arithmetic and copies ran while one was open for 12% of the time, Pallas kernels for 0%

profile of v1, /device:TPU:0, one launch (start us, length us, event | category | flops | bytes accessed | tf_op | source)
XLA Modules:
  0.0 1282.2 jit_solution(10702796396701222458)
XLA Ops:
  7.4 26.6 %all_gather.66 = bf16[768,384]{1,0:T(8,128)(2,1)} all-gather(bf16[48,384]{1,0:T(8,128)(2,1)} %param.26), channel_id=1, replica_groups=mesh['ctx'=16,'fsdp'=2] {'ctx'}, dimensions={0}, use_global_device_ids=true | all-gather | bytes 626688 | tf_op jit(solution)/shard_map/all_gather | solution.py:149
  34.1 20.7 %all_gather.68 = bf16[768,384]{1,0:T(8,128)(2,1)} all-gather(bf16[48,384]{1,0:T(8,128)(2,1)} %param.27), channel_id=1, replica_groups=mesh['ctx'=16,'fsdp'=2] {'ctx'}, dimensions={0}, use_global_device_ids=true | all-gather | bytes 626688 | tf_op jit(solution)/shard_map/all_gather | solution.py:150
  54.8 22.2 %all_gather.63 = bf16[768,384]{1,0:T(8,128)(2,1)} all-gather(bf16[48,384]{1,0:T(8,128)(2,1)} %param.25), channel_id=1, replica_groups=mesh['ctx'=16,'fsdp'=2] {'ctx'}, dimensions={0}, use_global_device_ids=true | all-gather | bytes 626688 | tf_op jit(solution)/shard_map/all_gather | solution.py:148
  82.4 58.0 %all-reduce.10 = (bf16[768]{0:T(1024)(128)(2,1)S(1)}, bf16[768]{0:T(1024)(128)(2,1)S(1)}, bf16[3072]{0:T(1024)(128)(2,1)S(1)}, bf16[768]{0:T(1024)(128)(2,1)S(1)...) all-reduce(bf16[768]{0:T(1024)(128)(2,1)S(1)} %dynamic-update-slice, ...), channel_id=1, replica_groups=mesh['ctx'=16,'fsdp'=2] {'ctx'}, use_global_device_ids=true, to_apply=%add | all-reduce | flops 9216 | bytes 36864
  144.9 20.7 %all_gather.72 = bf16[768,384]{1,0:T(8,128)(2,1)} all-gather(bf16[48,384]{1,0:T(8,128)(2,1)S(1)} %copy-done.14), channel_id=1, replica_groups=mesh['ctx'=16,'fsdp'=2] {'ctx'}, dimensions={0}, use_global_device_ids=true | all-gather | bytes 626688 | tf_op jit(solution)/shard_map/all_gather | solution.py:151
  169.8 21.1 %all-gather.18.cloned.1.call-done = bf16[768,1536]{1,0:T(8,128)(2,1)} async-done(((bf16[48,1536]{1,0:T(8,128)(2,1)}), bf16[768,1536]{1,0:T(8,128)(2,1)}) %all-gather.18.cloned.1.call-update) | async-done | bytes 2359312 | tf_op jit(solution)/shard_map/all_gather | solution.py:152
  191.0 101.6 %all-gather.24.cloned.1.call-done = bf16[4096,1536]{1,0:T(8,128)(2,1)} async-done(((bf16[256,1536]{1,0:T(8,128)(2,1)}), bf16[4096,1536]{1,0:T(8,128)(2,1)}) %all-gather.24.cloned.1.call-update) | async-done | bytes 12582928 | tf_op jit(solution)/shard_map/all_gather | solution.py:210
  292.6 77.9 %while.36 = (s32[]{:T(128)}, bf16[1,256,768]{1,2,0:T(8,128)(2,1)S(1)}, f32[12,1,256]{2,1,0:T(1,128)S(1)}, bf16[1,256,768]{2,1,0:T(8,128)(2,1)S(1)}, bf16[1,4096,...) while((s32[]{:T(128)}, ...), condition=%wide.region_3.4_spmd.clone, body=%wide.region_0.3_spmd.clone.sunk | while | flops 276827904 | bytes 14829822 | solution.py:74
  316.1 2.7 fusion.148
  322.5 2.9 fusion.148
  329.2 2.8 fusion.148
  372.8 6.6 all-gather.20.cloned.1.call-done
  379.4 9.9 multiply_convert_fusion.1
  389.3 4.6 fusion.104
  397.4 6.1 convert_reduce_fusion
  407.8 6.1 broadcast_in_dim.102
  413.8 142.1 %while.37 = (s32[]{:T(128)}, bf16[1,256,768]{1,2,0:T(8,128)(2,1)S(1)}, bf16[1,4096,1536]{1,2,0:T(8,128)(2,1)}, bf16[1,256,768]{2,1,0:T(8,128)(2,1)S(1)}, bf16[1,...) while((s32[]{:T(128)}, ...), condition=%wide.region_14.15_spmd.clone, body=%wide.region_12.14_spmd.clone.sunk | while | flops 680808192 | bytes 37041444 | solution.py:116
  416.5 2.8 multiply_reduce_fusion.6
  428.4 2.7 multiply_reduce_fusion.6
  440.3 2.8 multiply_reduce_fusion.6
  452.1 2.7 multiply_reduce_fusion.6
  463.9 2.7 multiply_reduce_fusion.6
  475.7 2.7 multiply_reduce_fusion.6
  487.6 2.7 multiply_reduce_fusion.6
  499.4 2.7 multiply_reduce_fusion.6
  511.3 2.8 multiply_reduce_fusion.6
  523.1 2.8 multiply_reduce_fusion.6
  534.9 2.8 multiply_reduce_fusion.6
  546.8 2.8 multiply_reduce_fusion.6
  560.7 5.7 convolution_convert_fusion.1
  568.2 3.7 convolution_convert_fusion
  571.9 7.1 copy.50
  579.1 111.7 %reduce-scatter.24.cloned.1.call-done = bf16[1,256,1536]{1,2,0:T(8,128)(2,1)} async-done(((bf16[1,4096,1536]{1,2,0:T(8,128)(2,1)}), bf16[1,256,1536]{1,2,0:T(8,128)(2,1)}) %reduce-scatter.24.cloned.1.call-update) | async-done | bytes 786448 | tf_op jit(solution)/shard_map/reduce_scatter | solution.py:246
  693.4 20.4 %reduce-scatter.26.cloned.1.call-done = bf16[768,384]{0,1:T(8,128)(2,1)} async-done(((bf16[768,768]{0,1:T(8,128)(2,1)}), bf16[768,384]{0,1:T(8,128)(2,1)}) %reduce-scatter.26.cloned.1.call-update) | async-done | bytes 589840 | tf_op jit(solution)/shard_map/reduce_scatter | solution.py:272
  716.1 21.9 %reduce-scatter.46.cloned.1.call-done = bf16[384,768]{1,0:T(8,128)(2,1)} async-done(((bf16[768,768]{1,0:T(8,128)(2,1)}), bf16[384,768]{1,0:T(8,128)(2,1)}) %reduce-scatter.46.cloned.1.call-update) | async-done | bytes 589840
  740.2 60.0 %reduce-scatter.34.cloned.1.call-done = bf16[768,1536]{1,0:T(8,128)(2,1)} async-done(((bf16[768,3072]{1,0:T(8,128)(2,1)}), bf16[768,1536]{1,0:T(8,128)(2,1)}) %reduce-scatter.34.cloned.1.call-update) | async-done | bytes 2359312 | tf_op jit(solution)/shard_map/reduce_scatter | solution.py:284
  800.2 62.4 %reduce-scatter.48.cloned.1.call-done = bf16[384,3072]{1,0:T(8,128)(2,1)} async-done(((bf16[768,3072]{1,0:T(8,128)(2,1)}), bf16[384,3072]{1,0:T(8,128)(2,1)}) %reduce-scatter.48.cloned.1.call-update) | async-done | bytes 2359312
  862.6 4.4 copy.51
  868.6 17.9 %reduce-scatter.28.cloned.1.call-done = bf16[768,384]{0,1:T(8,128)(2,1)} async-done(((bf16[768,768]{0,1:T(8,128)(2,1)}), bf16[768,384]{0,1:T(8,128)(2,1)}) %reduce-scatter.28.cloned.1.call-update) | async-done | bytes 589840 | tf_op jit(solution)/shard_map/reduce_scatter | solution.py:275
  892.2 2.8 convolution_add_fusion.3
  895.0 50.1 %reduce-scatter.40.cloned.1.call-done = bf16[48,384]{1,0:T(8,128)(2,1)} async-done(((bf16[768,384]{1,0:T(8,128)(2,1)}), bf16[48,384]{1,0:T(8,128)(2,1)}) %reduce-scatter.40.cloned.1.call-update) | async-done | bytes 36880
  946.7 55.7 %reduce-scatter.32.cloned.1.call-done = bf16[48,384]{1,0:T(8,128)(2,1)} async-done(((bf16[768,384]{1,0:T(8,128)(2,1)}), bf16[48,384]{1,0:T(8,128)(2,1)}) %reduce-scatter.32.cloned.1.call-update) | async-done | bytes 36880 | tf_op jit(solution)/shard_map/reduce_scatter | solution.py:301
  1003.8 64.7 %reduce-scatter.36.cloned.1.call-done = bf16[48,1536]{1,0:T(8,128)(2,1)} async-done(((bf16[768,1536]{1,0:T(8,128)(2,1)}), bf16[48,1536]{1,0:T(8,128)(2,1)}) %reduce-scatter.36.cloned.1.call-update) | async-done | bytes 147472 | tf_op jit(solution)/shard_map/reduce_scatter | solution.py:304
  1070.2 64.0 %reduce-scatter.38.cloned.1.call-done = bf16[192,384]{1,0:T(8,128)(2,1)} async-done(((bf16[3072,384]{1,0:T(8,128)(2,1)}), bf16[192,384]{1,0:T(8,128)(2,1)}) %reduce-scatter.38.cloned.1.call-update) | async-done | bytes 147472 | tf_op jit(solution)/shard_map/reduce_scatter | solution.py:307
  1135.9 21.5 %reduce-scatter.30.cloned.1.call-done = bf16[768,384]{0,1:T(8,128)(2,1)} async-done(((bf16[768,768]{0,1:T(8,128)(2,1)}), bf16[768,384]{0,1:T(8,128)(2,1)}) %reduce-scatter.30.cloned.1.call-update) | async-done | bytes 589840 | tf_op jit(solution)/shard_map/reduce_scatter | solution.py:278
  1159.7 40.3 %all-reduce.9 = (f32[768]{0:T(1024)S(1)}, f32[768]{0:T(1024)S(1)}, f32[768]{0:T(1024)S(1)}, f32[768]{0:T(1024)S(1)}, f32[768]{0:T(1024)S(1)}, /*index=5*/f32[307...) all-reduce(f32[768]{0:T(1024)S(1)} %convert_reduce_fusion.4, ...), channel_id=1, replica_groups=mesh['ctx'=16,'fsdp'=2] {'ctx','fsdp'}, use_global_device_ids=true, to_apply=%region_29.30 | all-reduce | flops 9220 | bytes 73760 | tf_op jit(solution)/shard_map/psum | solution.py:319
  1209.0 6.7 reduce-scatter.42.cloned.1.call-done
  1217.3 56.3 %reduce-scatter.44.cloned.1.call-done = bf16[48,384]{1,0:T(8,128)(2,1)} async-done(((bf16[768,384]{1,0:T(8,128)(2,1)}), bf16[48,384]{1,0:T(8,128)(2,1)}) %reduce-scatter.44.cloned.1.call-update) | async-done | bytes 36880
  (364 shorter events, 240.2 us)
Async XLA Ops:
  7.2 71.1 %copy-start.33 = (u32[32]{0:T(128)S(1)}, u32[32]{0:T(128)}, u32[]{:S(2)}) copy-start(u32[32]{0:T(128)} %constant.311) | copy-start | bytes 388
  7.2 73.0 %copy-start.24 = (bf16[48]{0:T(256)(128)(2,1)S(1)}, bf16[48]{0:T(256)(128)(2,1)}, u32[]{:S(2)}) copy-start(bf16[48]{0:T(256)(128)(2,1)} %param.38) | copy-start | bytes 292
  7.2 73.2 %copy-start.25 = (bf16[48]{0:T(256)(128)(2,1)S(1)}, bf16[48]{0:T(256)(128)(2,1)}, u32[]{:S(2)}) copy-start(bf16[48]{0:T(256)(128)(2,1)} %param.37) | copy-start | bytes 292
  7.2 73.5 %copy-start.26 = (bf16[48]{0:T(256)(128)(2,1)S(1)}, bf16[48]{0:T(256)(128)(2,1)}, u32[]{:S(2)}) copy-start(bf16[48]{0:T(256)(128)(2,1)} %param.34) | copy-start | bytes 292
  7.2 73.7 %copy-start.27 = (bf16[48]{0:T(256)(128)(2,1)S(1)}, bf16[48]{0:T(256)(128)(2,1)}, u32[]{:S(2)}) copy-start(bf16[48]{0:T(256)(128)(2,1)} %param.35) | copy-start | bytes 292
  7.2 73.9 %copy-start.28 = (bf16[48]{0:T(256)(128)(2,1)S(1)}, bf16[48]{0:T(256)(128)(2,1)}, u32[]{:S(2)}) copy-start(bf16[48]{0:T(256)(128)(2,1)} %param.33) | copy-start | bytes 292
  7.3 74.1 %copy-start.29 = (bf16[48]{0:T(256)(128)(2,1)S(1)}, bf16[48]{0:T(256)(128)(2,1)}, u32[]{:S(2)}) copy-start(bf16[48]{0:T(256)(128)(2,1)} %param.32) | copy-start | bytes 292
  7.3 74.4 %copy-start.30 = (bf16[48]{0:T(256)(128)(2,1)S(1)}, bf16[48]{0:T(256)(128)(2,1)}, u32[]{:S(2)}) copy-start(bf16[48]{0:T(256)(128)(2,1)} %param.31) | copy-start | bytes 292
  7.3 74.6 %copy-start.31 = (bf16[48]{0:T(256)(128)(2,1)S(1)}, bf16[48]{0:T(256)(128)(2,1)}, u32[]{:S(2)}) copy-start(bf16[48]{0:T(256)(128)(2,1)} %param.39) | copy-start | bytes 292
  7.3 74.8 %copy-start.32 = (bf16[192]{0:T(256)(128)(2,1)S(1)}, bf16[192]{0:T(256)(128)(2,1)}, u32[]{:S(2)}) copy-start(bf16[192]{0:T(256)(128)(2,1)} %param.36) | copy-start | bytes 1156
  7.3 133.1 %copy-start = (bf16[1,256,768]{2,1,0:T(8,128)(2,1)S(1)}, bf16[1,256,768]{2,1,0:T(8,128)(2,1)}, u32[]{:S(2)}) copy-start(bf16[1,256,768]{2,1,0:T(8,128)(2,1)} %param.22) | copy-start | bytes 1179652
  7.3 133.1 %all-gather.12.cloned.1.call-start = ((), (), s32[]{:S(2)}) async-start(), calls=%async_computation.14 | async-start | bytes 1769472 | tf_op jit(solution)/shard_map/all_gather | solution.py:182
  34.0 108.1 %all-gather.14.cloned.1.call-start = ((), (), s32[]{:S(2)}) async-start(), calls=%async_computation.15 | async-start | bytes 1769472 | tf_op jit(solution)/shard_map/all_gather | solution.py:183
  54.8 111.7 %all-gather.10.cloned.1.call-start = ((), (), s32[]{:S(2)}) async-start(), calls=%async_computation.13 | async-start | bytes 1769472 | tf_op jit(solution)/shard_map/all_gather | solution.py:181
  77.1 91.1 %all-gather.22.cloned.1.call-start = ((), (), s32[]{:S(2)}) async-start(), calls=%async_computation.19 | async-start | bytes 2506752 | tf_op jit(solution)/shard_map/all_gather | solution.py:153
  77.7 113.2 %all-gather.18.cloned.1.call-start = ((), (), s32[]{:S(2)}) async-start(), calls=%async_computation.17 | async-start | bytes 2506752 | tf_op jit(solution)/shard_map/all_gather | solution.py:152
  78.3 214.3 %all-gather.24.cloned.1.call-start = ((), (), s32[]{:S(2)}) async-start(), calls=%async_computation.28 | async-start | bytes 13369344 | tf_op jit(solution)/shard_map/all_gather | solution.py:210
  144.9 225.7 %all-gather.16.cloned.1.call-start = ((), (), s32[]{:S(2)}) async-start(), calls=%async_computation.16 | async-start | bytes 1769472 | tf_op jit(solution)/shard_map/all_gather | solution.py:184
  165.6 213.8 %all-gather.20.cloned.1.call-start = ((), (), s32[]{:S(2)}) async-start(), calls=%async_computation.18 | async-start | bytes 7077888 | tf_op jit(solution)/shard_map/all_gather | solution.py:185
  168.2 221.0 %collective-permute-start = (bf16[3072,384]{1,0:T(8,128)(2,1)}, bf16[3072,384]{1,0:T(8,128)(2,1)}, u32[]{:S(2)}, u32[]{:S(2)}) collective-permute-start(bf16[3072,384]{1,0:T(8,128)(2,1)} %all-gather.22.cloned.1.call-done), channel_id=1, source_target_pairs={{0,1},{1,0},{2,3},{3,2},{4,5},{5,4},{6,7},{7,6},{8,9},{9,8},{10,11... | collective-permute-start | bytes 7077896 | tf_op jit(solution)/shard_map/ppermute | solution.py:169
  190.9 499.9 %reduce-scatter.24.cloned.1.call-start = ((), (), s32[]{:S(2)}) async-start(), calls=%async_computation.20 | async-start | bytes 13369344 | tf_op jit(solution)/shard_map/reduce_scatter | solution.py:246
  370.5 18.7 %copy-start.4 = (bf16[1,256,768]{1,2,0:T(8,128)(2,1)}, bf16[1,256,768]{1,2,0:T(8,128)(2,1)S(1)}, u32[]{:S(2)}) copy-start(bf16[1,256,768]{1,2,0:T(8,128)(2,1)S(1)} %get-tuple-element.372) | copy-start | bytes 1179652
  372.8 33.1 %copy-start.18 = (f32[256]{0:T(256)}, f32[256]{0:T(256)S(1)}, u32[]{:S(2)}) copy-start(f32[256]{0:T(256)S(1)} %fusion.91) | copy-start | bytes 3076
  379.4 9.9 copy-start.23
  395.5 8.1 slice-start
  397.4 6.1 copy-start.9
  397.4 6.2 slice-start.1
  555.9 157.9 %reduce-scatter.26.cloned.1.call-start = ((), (), s32[]{:S(2)}) async-start(), calls=%async_computation.21 | async-start | bytes 1769472 | tf_op jit(solution)/shard_map/reduce_scatter | solution.py:272
  557.5 180.5 %reduce-scatter.46.cloned.1.call-start = ((), (), s32[]{:S(2)}) async-start(), calls=%async_computation.32 | async-start | bytes 1769472
  560.6 239.5 %reduce-scatter.34.cloned.1.call-start = ((), (), s32[]{:S(2)}) async-start(), calls=%async_computation.25 | async-start | bytes 7077888 | tf_op jit(solution)/shard_map/reduce_scatter | solution.py:284
  566.4 296.2 %reduce-scatter.48.cloned.1.call-start = ((), (), s32[]{:S(2)}) async-start(), calls=%async_computation.33 | async-start | bytes 7077888
  579.0 307.4 %reduce-scatter.28.cloned.1.call-start = ((), (), s32[]{:S(2)}) async-start(), calls=%async_computation.22 | async-start | bytes 1769472 | tf_op jit(solution)/shard_map/reduce_scatter | solution.py:275
  693.3 251.8 %reduce-scatter.40.cloned.1.call-start = ((), (), s32[]{:S(2)}) async-start(), calls=%async_computation.29 | async-start | bytes 626688
  716.0 286.4 %reduce-scatter.32.cloned.1.call-start = ((), (), s32[]{:S(2)}) async-start(), calls=%async_computation.24 | async-start | bytes 626688 | tf_op jit(solution)/shard_map/reduce_scatter | solution.py:301
  740.1 328.4 %reduce-scatter.36.cloned.1.call-start = ((), (), s32[]{:S(2)}) async-start(), calls=%async_computation.26 | async-start | bytes 2506752 | tf_op jit(solution)/shard_map/reduce_scatter | solution.py:304
  800.2 334.1 %reduce-scatter.38.cloned.1.call-start = ((), (), s32[]{:S(2)}) async-start(), calls=%async_computation.27 | async-start | bytes 2506752 | tf_op jit(solution)/shard_map/reduce_scatter | solution.py:307
  867.0 290.4 %reduce-scatter.30.cloned.1.call-start = ((), (), s32[]{:S(2)}) async-start(), calls=%async_computation.23 | async-start | bytes 1769472 | tf_op jit(solution)/shard_map/reduce_scatter | solution.py:278
  868.6 347.1 %reduce-scatter.42.cloned.1.call-start = ((), (), s32[]{:S(2)}) async-start(), calls=%async_computation.30 | async-start | bytes 626688
  888.6 385.0 %reduce-scatter.44.cloned.1.call-start = ((), (), s32[]{:S(2)}) async-start(), calls=%async_computation.31 | async-start | bytes 626688
  892.1 267.6 %copy-start.15 = (f32[768]{0:T(1024)S(1)}, f32[768]{0:T(1024)}, u32[]{:S(2)}) copy-start(f32[768]{0:T(1024)} %get-tuple-element.457) | copy-start | bytes 9220
  892.1 267.6 %copy-start.16 = (f32[768]{0:T(1024)S(1)}, f32[768]{0:T(1024)}, u32[]{:S(2)}) copy-start(f32[768]{0:T(1024)} %get-tuple-element.505) | copy-start | bytes 9220
  892.1 267.6 %copy-start.17 = (f32[768]{0:T(1024)S(1)}, f32[768]{0:T(1024)}, u32[]{:S(2)}) copy-start(f32[768]{0:T(1024)} %get-tuple-element.507) | copy-start | bytes 9220
  892.1 267.6 %copy-start.19 = (f32[3072]{0:T(1024)S(1)}, f32[3072]{0:T(1024)}, u32[]{:S(2)}) copy-start(f32[3072]{0:T(1024)} %get-tuple-element.528) | copy-start | bytes 36868
  892.2 267.6 %copy-start.21 = (f32[768]{0:T(1024)S(1)}, f32[768]{0:T(1024)}, u32[]{:S(2)}) copy-start(f32[768]{0:T(1024)} %get-tuple-element.446) | copy-start | bytes 9220
  892.2 267.6 %copy-start.22 = (f32[768]{0:T(1024)S(1)}, f32[768]{0:T(1024)}, u32[]{:S(2)}) copy-start(f32[768]{0:T(1024)} %get-tuple-element.451) | copy-start | bytes 9220
  892.2 315.0 %copy-start.2 = (bf16[768,768]{1,0:T(8,128)(2,1)S(1)}, bf16[768,768]{1,0:T(8,128)(2,1)}, u32[]{:S(2)}) copy-start(bf16[768,768]{1,0:T(8,128)(2,1)} %all-gather.12.cloned.1.call-done) | copy-start | bytes 3538948
  895.0 312.2 %copy-start.8 = (f32[256,768]{1,0:T(8,128)S(1)}, f32[256,768]{1,0:T(8,128)}, u32[]{:S(2)}) copy-start(f32[256,768]{1,0:T(8,128)} %convolution_add_fusion.3) | copy-start | bytes 2359300
  1200.1 7.6 copy-start.13
  (10 other events, 27.0 us)
Sparse Core Ops, SparseCore 0:
  34.1 20.0 all-gather.11
  55.8 22.7 all-gather.13
  80.1 22.7 all-gather.9
  105.1 42.6 all-gather.21
  149.9 40.9 all-gather.17
  193.0 99.5 all-gather.23
  294.1 20.9 all-gather.15
  316.7 62.6 all-gather.19
  556.0 134.7 reduce-scatter.23
  692.9 20.8 reduce-scatter.25
  716.2 21.7 reduce-scatter.45
  740.1 59.9 reduce-scatter.33
  802.5 59.9 reduce-scatter.47
  864.7 21.7 reduce-scatter.27
  890.3 54.7 reduce-scatter.39
  948.5 53.8 reduce-scatter.31
  1006.5 61.9 reduce-scatter.35
  1072.2 62.0 reduce-scatter.37
  1136.6 20.7 reduce-scatter.29
  1160.8 54.8 reduce-scatter.41
  1219.7 53.8 reduce-scatter.43
